TPU v7x, 128 devices: a whole 4x4x4 slice. The times are simulated.
128 devices in a mesh: pair: 8 (over x, core), ints: 16 (over y, z).
Axes of the slice: x: 4, y: 4, z: 4, core: 2. Of those that a mesh axis runs over, the one named last changes fastest.
Arguments:
- t2: bfloat16 [4096, 8192], P('pair', 'ints'), may hold values from -6 to 6
- t2_live: int32 [8, 64], P('pair', 'ints'), may hold values 0 or 1
- int_tiles: int32 [5120, 2], P('ints'), may hold values from 0 to 63
- integrals: bfloat16 [5120, 128, 128], P('ints'), may hold values from -0.0625 to 0.0625
- cycle_w: bfloat16 [4096, 4096], P('pair'), may hold values from -0.09375 to 0.09375
- res_live: int32 [8, 64], P('pair', 'ints'), may hold values 0 or 1
Outputs:
- residual: float32 [4096, 8192], P('pair', 'ints')
All inputs are finite; a program needn't handle non-finite values. No bound on the sum of `t2_live` or of `res_live` on one device may be relied on, other than what follows from the above.
Results may differ from a plain program's by a relative error of at most 0.0003.
Values may be sent and summed in bfloat16 or wider, within the bound.
No kernel may reach another device: no remote copies, remote signals or barrier semaphores. Data moves between devices by JAX's collectives and lax.ppermute only.
A program may use at most 192 MiB of HBM per device.

v0:
```python
import jax
import jax.numpy as jnp
from jax import lax
from jax.sharding import PartitionSpec as P


def local(t2, t2_live, int_tiles, integrals, cycle_w, res_live):
    rows_here = t2.shape[0]
    tile_size = integrals.shape[1]
    tiles_here = t2.shape[1] // tile_size
    live_mask = t2_live[0].astype(t2.dtype)
    amps = (t2.reshape(rows_here, tiles_here, tile_size) * live_mask[None, :, None]).reshape(
        rows_here, tiles_here * tile_size
    )
    block_amps = lax.all_gather(amps, "ints", axis=1, tiled=True)
    tiles_all = block_amps.shape[1] // tile_size
    amps_tiled = block_amps.reshape(rows_here, tiles_all, tile_size)
    count_here = integrals.shape[0]
    group_size = 64
    tile_groups = int_tiles.reshape(count_here // group_size, group_size, 2)
    int_groups = integrals.reshape(count_here // group_size, group_size, tile_size, tile_size)
    tile_ids = jnp.arange(tiles_all, dtype=jnp.int32)

    def ladder_step(partial_value, entry):
        pairs_uv, blocks = entry
        source_table = (pairs_uv[:, 0:1] == tile_ids[None, :]).astype(jnp.bfloat16)
        target_table = (pairs_uv[:, 1:2] == tile_ids[None, :]).astype(jnp.float32)
        picked = jnp.einsum(
            "jt,ptc->jpc", source_table, amps_tiled, preferred_element_type=jnp.float32
        ).astype(jnp.bfloat16)
        product = jnp.einsum("jpc,jcd->jpd", picked, blocks, preferred_element_type=jnp.float32)
        partial_value = partial_value + jnp.einsum(
            "jv,jpd->vpd", target_table, product, precision=lax.Precision.HIGHEST
        )
        return (partial_value, None)

    start_sum = jnp.zeros((tiles_all, rows_here, tile_size), jnp.float32)
    partial_value, _ = lax.scan(ladder_step, start_sum, (tile_groups, int_groups))
    summed = lax.psum(partial_value, "ints")
    owned = lax.dynamic_slice_in_dim(summed, lax.axis_index("ints") * tiles_here, tiles_here, 0)
    ladder = owned.transpose(1, 0, 2).reshape(rows_here, tiles_here * tile_size)
    cycle_term = jnp.dot(
        cycle_w,
        lax.all_gather(amps, "pair", axis=0, tiled=True),
        preferred_element_type=jnp.float32,
    )
    keep_mask = jnp.repeat(res_live[0], tile_size).astype(jnp.float32)[None, :]
    return keep_mask * (ladder + cycle_term)


def solution(mesh):
    placed = (
        P("pair", "ints"),
        P("pair", "ints"),
        P("ints", None),
        P("ints", None, None),
        P("pair", None),
        P("pair", "ints"),
    )
    return jax.shard_map(
        local, mesh=mesh, in_specs=placed, out_specs=P("pair", "ints"), check_vma=False
    )
```

profile of v0, /device:TPU:1, one launch (start us, length us, event | category | flops | bytes accessed | tf_op | source)
XLA Modules:
  0.0 551.5 jit_solution(12331240370962497261)
XLA Ops:
  7.4 0.0 all-gather.3.cloned.1.call-start
  7.4 0.7 convert_bitcast_fusion
  8.0 0.1 broadcast_bitcast_fusion.1
  8.1 1.9 broadcast_multiply_fusion
  10.0 0.0 all-gather.3.cloned.1.call-update
  10.0 0.0 all-reduce.2.cloned.1.call-start
  10.1 0.8 reshape.30
  10.8 80.4 %all-gather.3.cloned.1.call-done = bf16[512,8192]{1,0:T(8,128)(2,1)} async-done(((bf16[512,512]{1,0:T(8,128)(2,1)}), bf16[512,8192]{1,0:T(8,128)(2,1)}) %all-gather.3.cloned.1.call-update) | async-done | bytes 8388624 | tf_op jit(solution)/shard_map/all_gather | solution.py:15
  91.2 9.3 %copy.15 = bf16[64,8,64,128]{3,2,1,0:T(8,128)(2,1)} copy(bf16[64,8,64,128]{3,1,2,0:T(8,128)(2,1)} %bitcast.55) | data formatting | bytes 16777216
  100.5 213.6 %while.12 = (s32[]{:T(128)}, f32[64,512,128]{2,0,1:T(8,128)}, s32[5,64,2]{1,0,2:T(8,128)S(1)}, bf16[512,64,128]{2,1,0:T(8,128)(2,1)}, bf16[5,64,128,128]{3,2,1,0:T(8,128)(2,1)}, /*index=5*/s32[]{:T(128)}, s32[]{:T(128)}) while((s32[]{:T(128)}, f32[64,512,128]{2,0,1:T(8,128)}, s32[5,64,2]{1,0,2:T(8,128)S(1)}, ...), condition=%wide.region_1.2_spmd.clone.clone, body=%wide.region_0.1_spmd.clone.clone.sunk | while | flops 4840235008 | bytes 94374496 | solution.py:38
  100.5 5.8 %fusion.34 = bf16[64,512,128]{2,0,1:T(8,128)(2,1)S(1)} fusion(bf16[512,64,128]{2,1,0:T(8,128)(2,1)} %get-tuple-element.146, s32[64]{0:T(128)S(1)} %get-tuple-element.127), kind=kOutput, calls=%fused_computation.12.clone.1 | convolution fusion | flops 536875008 | bytes 16777472 | tf_op jit(solution)/shard_map/while/body/eval_jaxpr/jt,ptc->jpc/dot_general | solution.py:28
  106.3 13.9 %fusion.35 = f32[64,512,128]{2,1,0:T(8,128)} fusion(bf16[64,512,128]{2,0,1:T(8,128)(2,1)S(1)} %fusion.34, bf16[5,64,128,128]{3,2,1,0:T(8,128)(2,1)} %get-tuple-element.147, s32[]{:T(128)S(6)} %copy.28), kind=kOutput, calls=%fused_computation.5.clone.1 | convolution fusion | flops 1073741824 | bytes 27262980 | tf_op jit(solution)/shard_map/while/body/eval_jaxpr/jpc,jcd->jpd/dot_general | solution.py:31
  120.2 20.4 %select_add_fusion.2 = f32[64,512,128]{2,0,1:T(8,128)} fusion(f32[64,512,128]{2,0,1:T(8,128)} %get-tuple-element.137, f32[64,512,128]{2,1,0:T(8,128)} %fusion.35, pred[]{:T(512)S(6)} %compare.3, s32[64]{0:T(128)S(1)} %get-tuple-element.128), kind=kOutput, calls=%fused_computation.4.clone.1 | convolution fusion | flops 3229618176 | bytes 50331904 | tf_op jit(solution)/shard_map/while/body/eval_jaxpr/jv,jpd->vpd/dot_general | solution.py:32
  140.6 5.8 %fusion.34 = bf16[64,512,128]{2,0,1:T(8,128)(2,1)S(1)} fusion(bf16[512,64,128]{2,1,0:T(8,128)(2,1)} %get-tuple-element.146, s32[64]{0:T(128)S(1)} %get-tuple-element.127), kind=kOutput, calls=%fused_computation.12.clone.1 | convolution fusion | flops 536875008 | bytes 16777472 | tf_op jit(solution)/shard_map/while/body/eval_jaxpr/jt,ptc->jpc/dot_general | solution.py:28
  146.4 13.9 %fusion.35 = f32[64,512,128]{2,1,0:T(8,128)} fusion(bf16[64,512,128]{2,0,1:T(8,128)(2,1)S(1)} %fusion.34, bf16[5,64,128,128]{3,2,1,0:T(8,128)(2,1)} %get-tuple-element.147, s32[]{:T(128)S(6)} %copy.28), kind=kOutput, calls=%fused_computation.5.clone.1 | convolution fusion | flops 1073741824 | bytes 27262980 | tf_op jit(solution)/shard_map/while/body/eval_jaxpr/jpc,jcd->jpd/dot_general | solution.py:31
  160.3 23.7 %select_add_fusion.2 = f32[64,512,128]{2,0,1:T(8,128)} fusion(f32[64,512,128]{2,0,1:T(8,128)} %get-tuple-element.137, f32[64,512,128]{2,1,0:T(8,128)} %fusion.35, pred[]{:T(512)S(6)} %compare.3, s32[64]{0:T(128)S(1)} %get-tuple-element.128), kind=kOutput, calls=%fused_computation.4.clone.1 | convolution fusion | flops 3229618176 | bytes 50331904 | tf_op jit(solution)/shard_map/while/body/eval_jaxpr/jv,jpd->vpd/dot_general | solution.py:32
  184.0 5.8 %fusion.34 = bf16[64,512,128]{2,0,1:T(8,128)(2,1)S(1)} fusion(bf16[512,64,128]{2,1,0:T(8,128)(2,1)} %get-tuple-element.146, s32[64]{0:T(128)S(1)} %get-tuple-element.127), kind=kOutput, calls=%fused_computation.12.clone.1 | convolution fusion | flops 536875008 | bytes 16777472 | tf_op jit(solution)/shard_map/while/body/eval_jaxpr/jt,ptc->jpc/dot_general | solution.py:28
  189.8 13.9 %fusion.35 = f32[64,512,128]{2,1,0:T(8,128)} fusion(bf16[64,512,128]{2,0,1:T(8,128)(2,1)S(1)} %fusion.34, bf16[5,64,128,128]{3,2,1,0:T(8,128)(2,1)} %get-tuple-element.147, s32[]{:T(128)S(6)} %copy.28), kind=kOutput, calls=%fused_computation.5.clone.1 | convolution fusion | flops 1073741824 | bytes 27262980 | tf_op jit(solution)/shard_map/while/body/eval_jaxpr/jpc,jcd->jpd/dot_general | solution.py:31
  203.7 23.7 %select_add_fusion.2 = f32[64,512,128]{2,0,1:T(8,128)} fusion(f32[64,512,128]{2,0,1:T(8,128)} %get-tuple-element.137, f32[64,512,128]{2,1,0:T(8,128)} %fusion.35, pred[]{:T(512)S(6)} %compare.3, s32[64]{0:T(128)S(1)} %get-tuple-element.128), kind=kOutput, calls=%fused_computation.4.clone.1 | convolution fusion | flops 3229618176 | bytes 50331904 | tf_op jit(solution)/shard_map/while/body/eval_jaxpr/jv,jpd->vpd/dot_general | solution.py:32
  227.4 5.8 %fusion.34 = bf16[64,512,128]{2,0,1:T(8,128)(2,1)S(1)} fusion(bf16[512,64,128]{2,1,0:T(8,128)(2,1)} %get-tuple-element.146, s32[64]{0:T(128)S(1)} %get-tuple-element.127), kind=kOutput, calls=%fused_computation.12.clone.1 | convolution fusion | flops 536875008 | bytes 16777472 | tf_op jit(solution)/shard_map/while/body/eval_jaxpr/jt,ptc->jpc/dot_general | solution.py:28
  233.1 13.9 %fusion.35 = f32[64,512,128]{2,1,0:T(8,128)} fusion(bf16[64,512,128]{2,0,1:T(8,128)(2,1)S(1)} %fusion.34, bf16[5,64,128,128]{3,2,1,0:T(8,128)(2,1)} %get-tuple-element.147, s32[]{:T(128)S(6)} %copy.28), kind=kOutput, calls=%fused_computation.5.clone.1 | convolution fusion | flops 1073741824 | bytes 27262980 | tf_op jit(solution)/shard_map/while/body/eval_jaxpr/jpc,jcd->jpd/dot_general | solution.py:31
  247.1 23.7 %select_add_fusion.2 = f32[64,512,128]{2,0,1:T(8,128)} fusion(f32[64,512,128]{2,0,1:T(8,128)} %get-tuple-element.137, f32[64,512,128]{2,1,0:T(8,128)} %fusion.35, pred[]{:T(512)S(6)} %compare.3, s32[64]{0:T(128)S(1)} %get-tuple-element.128), kind=kOutput, calls=%fused_computation.4.clone.1 | convolution fusion | flops 3229618176 | bytes 50331904 | tf_op jit(solution)/shard_map/while/body/eval_jaxpr/jv,jpd->vpd/dot_general | solution.py:32
  270.7 5.8 %fusion.34 = bf16[64,512,128]{2,0,1:T(8,128)(2,1)S(1)} fusion(bf16[512,64,128]{2,1,0:T(8,128)(2,1)} %get-tuple-element.146, s32[64]{0:T(128)S(1)} %get-tuple-element.127), kind=kOutput, calls=%fused_computation.12.clone.1 | convolution fusion | flops 536875008 | bytes 16777472 | tf_op jit(solution)/shard_map/while/body/eval_jaxpr/jt,ptc->jpc/dot_general | solution.py:28
  276.5 13.9 %fusion.35 = f32[64,512,128]{2,1,0:T(8,128)} fusion(bf16[64,512,128]{2,0,1:T(8,128)(2,1)S(1)} %fusion.34, bf16[5,64,128,128]{3,2,1,0:T(8,128)(2,1)} %get-tuple-element.147, s32[]{:T(128)S(6)} %copy.28), kind=kOutput, calls=%fused_computation.5.clone.1 | convolution fusion | flops 1073741824 | bytes 27262980 | tf_op jit(solution)/shard_map/while/body/eval_jaxpr/jpc,jcd->jpd/dot_general | solution.py:31
  290.4 23.7 %select_add_fusion.2 = f32[64,512,128]{2,0,1:T(8,128)} fusion(f32[64,512,128]{2,0,1:T(8,128)} %get-tuple-element.137, f32[64,512,128]{2,1,0:T(8,128)} %fusion.35, pred[]{:T(512)S(6)} %compare.3, s32[64]{0:T(128)S(1)} %get-tuple-element.128), kind=kOutput, calls=%fused_computation.4.clone.1 | convolution fusion | flops 3229618176 | bytes 50331904 | tf_op jit(solution)/shard_map/while/body/eval_jaxpr/jv,jpd->vpd/dot_general | solution.py:32
  314.1 0.0 copy-start
  314.1 0.0 all-reduce.2.cloned.1.call-update
  314.1 0.2 all-gather.5.cloned.1.call-start
  314.4 0.3 all-gather.5.cloned.1.call-update
  314.7 0.0 copy-done
  314.8 0.1 broadcast_bitcast_fusion
  314.8 219.9 %all-reduce.2.cloned.1.call-done = f32[64,512,128]{2,0,1:T(8,128)} async-done(((f32[64,512,128]{2,0,1:T(8,128)}), f32[64,512,128]{2,0,1:T(8,128)}) %all-reduce.2.cloned.1.call-update) | async-done | bytes 16777232 | tf_op jit(solution)/shard_map/psum | solution.py:39
  534.7 1.8 dynamic-slice_bitcast_fusion
  536.5 0.4 copy.10
  536.9 0.0 all-gather.5.cloned.1.call-done
  536.9 5.8 %fusion.18 = f32[512,512]{0,1:T(8,128)S(1)} fusion(f32[512,512]{0,1:T(8,128)S(1)} %bitcast.56, bf16[4096,512]{1,0:T(8,128)(2,1)} %all-gather.5.cloned.1.call-done, bf16[512,4096]{1,0:T(8,128)(2,1)} %param.12, f32[512]{0:T(512)S(1)} %broadcast_bitcast_fusion), kind=kOutput, calls=%fused_computation.21 | convolution fusion | flops 2148007936 | bytes 10487808 | tf_op jit(solution)/shard_map/dot_general | solution.py:42
  542.8 1.3 copy.11
  (12 shorter events, 0.1 us)
Async XLA Ops:
  7.4 83.8 %all-gather.3.cloned.1.call-start = ((), (), s32[]{:S(2)}) async-start(), calls=%async_computation | async-start | bytes 8912896 | tf_op jit(solution)/shard_map/all_gather | solution.py:15
  10.0 524.7 %all-reduce.2.cloned.1.call-start = ((), (), s32[]{:S(2)}) async-start(), calls=%async_computation.1 | async-start | bytes 33554432 | tf_op jit(solution)/shard_map/psum | solution.py:39
  314.1 0.7 copy-start
  314.1 222.8 %all-gather.5.cloned.1.call-start = ((), (), s32[]{:S(2)}) async-start(), calls=%async_computation.2 | async-start | bytes 4718592 | tf_op jit(solution)/shard_map/all_gather | solution.py:44
Sparse Core Ops, SparseCore 0:
  10.3 80.8 all-gather.2
  314.2 220.4 all-reduce.1
Sparse Core Ops, SparseCore 1:
  316.3 32.4 all-gather.4
where the time goes:
time: 552 us
  waiting for transfers between devices  301 us (55%)
  matrix products  219 us (40%)
  between operations  14.9 us (3%)
  local copies, waits for them, and re-layouts  13.7 us (2%)
    psum x1, waiting for transfers between devices, local(): summed = lax.psum(partial_value, 'ints')  220 us
    dot_general x5, matrix products, ladder_step(): jnp.einsum('jv,jpd->vpd', target_table, product, precision=lax.Precision....  115 us
    all_gather x1, waiting for transfers between devices, local(): block_amps = lax.all_gather(amps, 'ints', axis=1, tiled=True)  80.4 us
    dot_general x5, matrix products, ladder_step(): jnp.einsum('jpc,jcd->jpd', picked, blocks, preferred_element_type=jnp.flo...  69.7 us
    dot_general x5, matrix products, ladder_step(): jnp.einsum('jt,ptc->jpc', source_table, amps_tiled, preferred_element_typ...  28.8 us
  transfers between devices with their start and end apart: 3, of which 2 were waited for; matrix products, arithmetic and copies ran while one was open for 1% of the time, Pallas kernels for 0%

commit v1 on v0

--- a/solution.py
+++ b/solution.py
@@ -12,7 +12,9 @@
     amps = (t2.reshape(rows_here, tiles_here, tile_size) * live_mask[None, :, None]).reshape(
         rows_here, tiles_here * tile_size
     )
-    block_amps = lax.all_gather(amps, "ints", axis=1, tiled=True)
+    block_amps = jnp.concatenate(
+        lax.all_to_all(jnp.stack([amps] * lax.axis_size("ints")), "ints", 0, 0), axis=1
+    )
     tiles_all = block_amps.shape[1] // tile_size
     amps_tiled = block_amps.reshape(rows_here, tiles_all, tile_size)
     count_here = integrals.shape[0]

time: 552 us -> 649 us (1.18)
  waiting for transfers between devices: 301 us -> 371 us
  local copies, waits for them, and re-layouts: 13.7 us -> 32.2 us
  starting transfers between devices: 0.27 us -> 9.05 us
    all_to_all x0 -> x1, waiting for transfers between devices: none -> 146 us  [local(): lax.all_to_all(jnp.stack([amps] * lax.axis_size('ints')), 'ints', 0, 0)]
    all_gather x1 -> x0, waiting for transfers between devices: 80.4 us -> none  [local(): block_amps = lax.all_gather(amps, 'ints', axis=1, tiled=True)]
    all_to_all x0 -> x1, local copies, waits for them, and re-layouts: none -> 12.3 us  [local(): lax.all_to_all(jnp.stack([amps] * lax.axis_size('ints')), 'ints', 0, 0)]
    all_to_all x0 -> x1, starting transfers between devices: none -> 8.78 us  [local(): lax.all_to_all(jnp.stack([amps] * lax.axis_size('ints')), 'ints', 0, 0)]
  transfers between devices with their start and end apart: 3 -> 3, of which waited for: 2 -> 2; matrix products, arithmetic and copies ran while one was open for 1% -> 0% of each run, Pallas kernels for 0% -> 0%
where the time goes in v1:
time: 649 us; the launch traced here: 648 us
  waiting for transfers between devices  371 us (57%)
  matrix products  220 us (34%)
  local copies, waits for them, and re-layouts  32.2 us (5%)
  between operations  14.9 us (2%)
  starting transfers between devices  9.05 us (1%)
    psum x1, waiting for transfers between devices, local(): summed = lax.psum(partial_value, 'ints')  224 us
    all_to_all x1, waiting for transfers between devices, local(): lax.all_to_all(jnp.stack([amps] * lax.axis_size('ints')), 'ints', 0, 0)  146 us
    dot_general x5, matrix products, ladder_step(): jnp.einsum('jv,jpd->vpd', target_table, product, precision=lax.Precision....  115 us
    dot_general x5, matrix products, ladder_step(): jnp.einsum('jpc,jcd->jpd', picked, blocks, preferred_element_type=jnp.flo...  69.9 us
    dot_general x5, matrix products, ladder_step(): jnp.einsum('jt,ptc->jpc', source_table, amps_tiled, preferred_element_typ...  28.8 us
  transfers between devices with their start and end apart: 3, of which 2 were waited for; matrix products, arithmetic and copies ran while one was open for 0% of the time, Pallas kernels for 0%

profile of v1, /device:TPU:1, one launch (start us, length us, event | category | flops | bytes accessed | tf_op | source)
XLA Modules:
  0.0 648.3 jit_solution(3241296732083674341)
XLA Ops:
  7.4 0.7 convert_bitcast_fusion
  8.0 0.1 broadcast_bitcast_fusion.1
  8.1 1.1 broadcast_multiply_fusion
  9.2 0.0 copy-start
  9.2 4.0 stack.3
  13.2 0.0 copy-start.1
  13.2 0.0 copy-done
  13.2 8.8 %all-to-all-start = ((bf16[16,512,512]{2,1,0:T(8,128)(2,1)}), bf16[16,512,512]{2,1,0:T(8,128)(2,1)}, u32[]{:S(2)}, u32[]{:S(2)}) async-start(bf16[16,512,512]{2,1,0:T(8,128)(2,1)} %stack.3), calls=%async_computation | async-start | bytes 16777216 | tf_op jit(solution)/shard_map/all_to_all | solution.py:16
  22.0 0.0 all-reduce.2.cloned.1.call-start
  22.1 0.0 copy-done.1
  22.1 0.1 reshape.33
  22.2 146.0 %all-to-all-done = bf16[16,512,512]{2,1,0:T(8,128)(2,1)} async-done(((bf16[16,512,512]{2,1,0:T(8,128)(2,1)}), bf16[16,512,512]{2,1,0:T(8,128)(2,1)}, u32[]{:S(2)}, u32[]{:S(2)}) %all-to-all-start) | async-done | bytes 8388640 | tf_op jit(solution)/shard_map/all_to_all | solution.py:16
  168.2 12.3 %copy.21 = bf16[16,512,512]{1,2,0:T(8,128)(2,1)} copy(bf16[16,512,512]{2,1,0:T(8,128)(2,1)} %all-to-all-done) | data formatting | bytes 16777216 | tf_op jit(solution)/shard_map/all_to_all | solution.py:16
  180.5 12.0 %copy.23 = bf16[512,64,128]{2,1,0:T(8,128)(2,1)} copy(bf16[512,64,128]{0,2,1:T(8,128)(2,1)} %bitcast.54) | data formatting | bytes 16777216
  192.6 213.9 %while.12 = (s32[]{:T(128)}, f32[64,512,128]{2,0,1:T(8,128)}, s32[5,64,2]{1,0,2:T(8,128)S(1)}, bf16[512,64,128]{2,1,0:T(8,128)(2,1)}, bf16[5,64,128,128]{3,2,1,0:T(8,128)(2,1)}, /*index=5*/s32[]{:T(128)}, s32[]{:T(128)}) while((s32[]{:T(128)}, f32[64,512,128]{2,0,1:T(8,128)}, s32[5,64,2]{1,0,2:T(8,128)S(1)}, ...), condition=%wide.region_1.2_spmd.clone.clone, body=%wide.region_0.1_spmd.clone.clone.sunk | while | flops 4844429312 | bytes 94374496 | solution.py:40
  192.6 5.8 convolution_convert_fusion.2
  198.3 14.0 %fusion.35 = f32[64,512,128]{2,1,0:T(8,128)} fusion(bf16[64,512,128]{2,0,1:T(8,128)(2,1)S(1)} %convolution_convert_fusion.2, bf16[5,64,128,128]{3,2,1,0:T(8,128)(2,1)} %get-tuple-element.157, s32[]{:T(128)S(6)} %copy.41), kind=kOutput, calls=%fused_computation.4.clone.1 | convolution fusion | flops 1073741824 | bytes 27262980 | tf_op jit(solution)/shard_map/while/body/eval_jaxpr/jpc,jcd->jpd/dot_general | solution.py:33
  212.3 20.4 %select_add_fusion.2 = f32[64,512,128]{2,0,1:T(8,128)} fusion(f32[64,512,128]{2,0,1:T(8,128)} %get-tuple-element.147, f32[64,512,128]{2,1,0:T(8,128)} %fusion.35, pred[]{:T(512)S(6)} %compare.3, s32[64]{0:T(128)S(1)} %get-tuple-element.138), kind=kOutput, calls=%fused_computation.3.clone.1 | convolution fusion | flops 3229618176 | bytes 50331904 | tf_op jit(solution)/shard_map/while/body/eval_jaxpr/jv,jpd->vpd/dot_general | solution.py:34
  232.7 5.8 convolution_convert_fusion.2
  238.5 14.0 %fusion.35 = f32[64,512,128]{2,1,0:T(8,128)} fusion(bf16[64,512,128]{2,0,1:T(8,128)(2,1)S(1)} %convolution_convert_fusion.2, bf16[5,64,128,128]{3,2,1,0:T(8,128)(2,1)} %get-tuple-element.157, s32[]{:T(128)S(6)} %copy.41), kind=kOutput, calls=%fused_computation.4.clone.1 | convolution fusion | flops 1073741824 | bytes 27262980 | tf_op jit(solution)/shard_map/while/body/eval_jaxpr/jpc,jcd->jpd/dot_general | solution.py:33
  252.5 23.7 %select_add_fusion.2 = f32[64,512,128]{2,0,1:T(8,128)} fusion(f32[64,512,128]{2,0,1:T(8,128)} %get-tuple-element.147, f32[64,512,128]{2,1,0:T(8,128)} %fusion.35, pred[]{:T(512)S(6)} %compare.3, s32[64]{0:T(128)S(1)} %get-tuple-element.138), kind=kOutput, calls=%fused_computation.3.clone.1 | convolution fusion | flops 3229618176 | bytes 50331904 | tf_op jit(solution)/shard_map/while/body/eval_jaxpr/jv,jpd->vpd/dot_general | solution.py:34
  276.2 5.8 convolution_convert_fusion.2
  281.9 14.0 %fusion.35 = f32[64,512,128]{2,1,0:T(8,128)} fusion(bf16[64,512,128]{2,0,1:T(8,128)(2,1)S(1)} %convolution_convert_fusion.2, bf16[5,64,128,128]{3,2,1,0:T(8,128)(2,1)} %get-tuple-element.157, s32[]{:T(128)S(6)} %copy.41), kind=kOutput, calls=%fused_computation.4.clone.1 | convolution fusion | flops 1073741824 | bytes 27262980 | tf_op jit(solution)/shard_map/while/body/eval_jaxpr/jpc,jcd->jpd/dot_general | solution.py:33
  295.9 23.7 %select_add_fusion.2 = f32[64,512,128]{2,0,1:T(8,128)} fusion(f32[64,512,128]{2,0,1:T(8,128)} %get-tuple-element.147, f32[64,512,128]{2,1,0:T(8,128)} %fusion.35, pred[]{:T(512)S(6)} %compare.3, s32[64]{0:T(128)S(1)} %get-tuple-element.138), kind=kOutput, calls=%fused_computation.3.clone.1 | convolution fusion | flops 3229618176 | bytes 50331904 | tf_op jit(solution)/shard_map/while/body/eval_jaxpr/jv,jpd->vpd/dot_general | solution.py:34
  319.6 5.8 convolution_convert_fusion.2
  325.4 14.0 %fusion.35 = f32[64,512,128]{2,1,0:T(8,128)} fusion(bf16[64,512,128]{2,0,1:T(8,128)(2,1)S(1)} %convolution_convert_fusion.2, bf16[5,64,128,128]{3,2,1,0:T(8,128)(2,1)} %get-tuple-element.157, s32[]{:T(128)S(6)} %copy.41), kind=kOutput, calls=%fused_computation.4.clone.1 | convolution fusion | flops 1073741824 | bytes 27262980 | tf_op jit(solution)/shard_map/while/body/eval_jaxpr/jpc,jcd->jpd/dot_general | solution.py:33
  339.4 23.7 %select_add_fusion.2 = f32[64,512,128]{2,0,1:T(8,128)} fusion(f32[64,512,128]{2,0,1:T(8,128)} %get-tuple-element.147, f32[64,512,128]{2,1,0:T(8,128)} %fusion.35, pred[]{:T(512)S(6)} %compare.3, s32[64]{0:T(128)S(1)} %get-tuple-element.138), kind=kOutput, calls=%fused_computation.3.clone.1 | convolution fusion | flops 3229618176 | bytes 50331904 | tf_op jit(solution)/shard_map/while/body/eval_jaxpr/jv,jpd->vpd/dot_general | solution.py:34
  363.1 5.8 convolution_convert_fusion.2
  368.8 14.0 %fusion.35 = f32[64,512,128]{2,1,0:T(8,128)} fusion(bf16[64,512,128]{2,0,1:T(8,128)(2,1)S(1)} %convolution_convert_fusion.2, bf16[5,64,128,128]{3,2,1,0:T(8,128)(2,1)} %get-tuple-element.157, s32[]{:T(128)S(6)} %copy.41), kind=kOutput, calls=%fused_computation.4.clone.1 | convolution fusion | flops 1073741824 | bytes 27262980 | tf_op jit(solution)/shard_map/while/body/eval_jaxpr/jpc,jcd->jpd/dot_general | solution.py:33
  382.8 23.7 %select_add_fusion.2 = f32[64,512,128]{2,0,1:T(8,128)} fusion(f32[64,512,128]{2,0,1:T(8,128)} %get-tuple-element.147, f32[64,512,128]{2,1,0:T(8,128)} %fusion.35, pred[]{:T(512)S(6)} %compare.3, s32[64]{0:T(128)S(1)} %get-tuple-element.138), kind=kOutput, calls=%fused_computation.3.clone.1 | convolution fusion | flops 3229618176 | bytes 50331904 | tf_op jit(solution)/shard_map/while/body/eval_jaxpr/jv,jpd->vpd/dot_general | solution.py:34
  406.5 0.0 copy-start.2
  406.5 0.0 all-reduce.2.cloned.1.call-update
  406.5 0.2 all-gather.2.cloned.1.call-start
  406.7 0.3 all-gather.2.cloned.1.call-update
  407.1 0.0 copy-done.2
  407.1 0.1 broadcast_bitcast_fusion
  407.2 224.3 %all-reduce.2.cloned.1.call-done = f32[64,512,128]{2,0,1:T(8,128)} async-done(((f32[64,512,128]{2,0,1:T(8,128)}), f32[64,512,128]{2,0,1:T(8,128)}) %all-reduce.2.cloned.1.call-update) | async-done | bytes 16777232 | tf_op jit(solution)/shard_map/psum | solution.py:41
  631.5 1.8 dynamic-slice_bitcast_fusion
  633.2 0.4 copy.24
  633.6 0.0 all-gather.2.cloned.1.call-done
  633.6 5.8 fusion.18
  639.5 1.3 copy.25
  (12 shorter events, 0.1 us)
Async XLA Ops:
  9.2 4.1 copy-start
  13.2 8.9 %copy-start.1 = (s32[320,2]{0,1:T(2,128)S(1)}, s32[320,2]{0,1:T(2,128)}, u32[]{:S(2)}) copy-start(s32[320,2]{0,1:T(2,128)} %param.10) | copy-start | bytes 7684
  13.2 154.9 %all-to-all-start = ((bf16[16,512,512]{2,1,0:T(8,128)(2,1)}), bf16[16,512,512]{2,1,0:T(8,128)(2,1)}, u32[]{:S(2)}, u32[]{:S(2)}) async-start(bf16[16,512,512]{2,1,0:T(8,128)(2,1)} %stack.3), calls=%async_computation | async-start | bytes 16777216 | tf_op jit(solution)/shard_map/all_to_all | solution.py:16
  22.0 609.4 %all-reduce.2.cloned.1.call-start = ((), (), s32[]{:S(2)}) async-start(), calls=%async_computation.1 | async-start | bytes 33554432 | tf_op jit(solution)/shard_map/psum | solution.py:41
  406.5 0.7 copy-start.2
  406.5 227.1 %all-gather.2.cloned.1.call-start = ((), (), s32[]{:S(2)}) async-start(), calls=%async_computation.2 | async-start | bytes 4718592 | tf_op jit(solution)/shard_map/all_gather | solution.py:46
Sparse Core Ops, SparseCore 0:
  406.6 224.8 all-reduce.1
Sparse Core Ops, SparseCore 1:
  408.7 36.8 all-gather.1
